TPU v7x, 256 devices: a whole 4x4x8 slice. The times are simulated.
256 devices in a mesh: sess: 32 (over y_hi, z, core), dp: 4 (over x), fsdp: 2 (over y_lo).
Axes of the slice: x: 4, y: 4 (y_hi: 2, y_lo: 2; y = y_hi * 2 + y_lo), z: 8, core: 2. Of those that a mesh axis runs over, the one named last changes fastest.
Arguments:
- unit_tokens: bfloat16 [4096, 128, 1024], P(('sess', 'dp', 'fsdp')), may hold values from -6 to 6
- block_owner: int32 [4096, 1], P(('sess', 'dp', 'fsdp')), may hold values from 0 to 31; in each aligned block of 16 rows (0 to 15, 16 to 31, ...) at most 2 rows name the same one
- block_clip: int32 [4096], P(('sess', 'dp', 'fsdp')), may hold values from 0 to 1
- block_valid: int32 [4096], P(('sess', 'dp', 'fsdp')), may hold values from 1 to 128, as said below
- latent_query_rows: bfloat16 [32, 1024], replicated, may hold values from -600 to 600
- latents: bfloat16 [32, 1024], replicated, may hold values from -1.5 to 1.5
- w_kv: bfloat16 [1024, 512], P('fsdp'), may hold values from -0.1875 to 0.1875
- w_out: bfloat16 [1024, 1024], P('fsdp'), may hold values from -0.75 to 0.75
- w_proj: bfloat16 [1024, 512], P('fsdp'), may hold values from -0.1875 to 0.1875
- movie_frame_embeddings: bfloat16 [512, 512], replicated, may hold values from -6 to 6
- clip_frame: int32 [512], P(('sess', 'dp', 'fsdp')), may hold values from 0 to 511
- logit_scale: float32 [1], replicated, may hold values from 40 to 60
Outputs:
- latent_state: bfloat16 [512, 32, 1024], P(('sess', 'dp', 'fsdp'))
- clip_loss: float32 [512], P(('sess', 'dp', 'fsdp'))
Inputs may be any that keep to these rules, and one draw needn't show every extreme that they name: `block_owner`: among the 16 blocks of one device no index is named more than 2 times, a bound that some block reaches. `block_valid`: the first block of every device is full.
All inputs are finite; a program needn't handle non-finite values.
Results may differ from a plain program's by a relative error of at most 0.009.
The roundings to bfloat16 on the way count: a program that leaves them out, or rounds other values in their place, can miss the bound.
Values may be sent and summed in bfloat16 or wider, within the bound.
A program may use at most 128 MiB of HBM per device.

v0:
```python
import math
import jax
import jax.numpy as jnp
from jax import lax
from jax.sharding import PartitionSpec as P

HEADS = 16
HEAD_DIM = 64
KV_HEADS = 4


def fold_rows(left, piece):
    return jnp.dot(left, piece, preferred_element_type=jnp.float32)


def keys_folded(left, weight):
    return fold_rows(left, lax.all_gather(weight, "fsdp", axis=0, tiled=True))


def output_folded(left, weight):
    return fold_rows(left, lax.all_gather(weight, "fsdp", axis=0, tiled=True))


def embed_folded(left, weight):
    return fold_rows(left, lax.all_gather(weight, "fsdp", axis=0, tiled=True))


def per_device(
    unit_tokens,
    block_owner,
    block_clip,
    block_valid,
    latent_query_rows,
    latents,
    w_kv,
    w_out,
    w_proj,
    movie_frame_embeddings,
    clip_frame,
    logit_scale,
):
    peers = lax.axis_size("sess")
    blocks_here, block_rows, width = unit_tokens.shape
    capacity = max(2, (2 * blocks_here + peers - 1) // peers)
    slots_all = peers * capacity
    kv_width = w_kv.shape[1] // 2
    group_size = HEADS // KV_HEADS
    clips_here = clip_frame.shape[0]
    lat_rows = latent_query_rows.shape[0]
    scaling = 1.0 / math.sqrt(HEAD_DIM)
    target = block_owner[:, 0]
    peer_hits = (target[:, None] == jnp.arange(peers, dtype=jnp.int32)[None, :]).astype(jnp.int32)
    preceding_value = jnp.cumsum(peer_hits, axis=0) - peer_hits
    rank_within = jnp.sum(preceding_value * peer_hits, axis=1)
    slot_of = target * capacity + rank_within
    placing = (slot_of[:, None] == jnp.arange(slots_all, dtype=jnp.int32)[None, :]).astype(
        jnp.bfloat16
    )
    meta_rows = jnp.stack([block_valid, block_clip], axis=1).astype(jnp.bfloat16)
    slot_meta = jnp.einsum("bs,bx->sx", placing, meta_rows, preferred_element_type=jnp.bfloat16)
    slot_meta = slot_meta.reshape(peers, capacity, 2)
    packed = jnp.einsum(
        "bs,bx->sx",
        placing,
        unit_tokens.reshape(blocks_here, block_rows * width),
        preferred_element_type=jnp.bfloat16,
    )
    packed = packed.reshape(peers, capacity, block_rows * width)
    arrived, arrived_meta = (
        lax.all_to_all(packed, "sess", split_axis=0, concat_axis=0, tiled=True),
        lax.all_to_all(slot_meta, "sess", split_axis=0, concat_axis=0, tiled=True),
    )
    kv_slots = keys_folded(arrived.reshape(slots_all * block_rows, width), w_kv).astype(
        jnp.bfloat16
    )
    kv_slots = kv_slots.reshape(slots_all, block_rows, 2 * kv_width)
    meta_float = arrived_meta.astype(jnp.float32).reshape(slots_all, 2)
    valid_count = meta_float[:, 0]
    slot_clip = meta_float[:, 1].astype(jnp.int32)
    row_live = jnp.arange(block_rows).astype(jnp.float32)[None, :] < valid_count[:, None]
    member = (slot_clip[None, :] == jnp.arange(clips_here, dtype=jnp.int32)[:, None]) & (
        valid_count[None, :] > 0.0
    )
    member_float = member.astype(jnp.float32)
    keys = kv_slots[:, :, :kv_width].reshape(slots_all, block_rows, KV_HEADS, HEAD_DIM)
    value_rows = kv_slots[:, :, kv_width:].reshape(slots_all, block_rows, KV_HEADS, HEAD_DIM)
    query = latent_query_rows.reshape(lat_rows, HEADS, HEAD_DIM)
    head_parts = []
    for head_position in range(HEADS):
        key_value_head = head_position // group_size
        scores = (
            jnp.einsum(
                "wa,pha->wph",
                query[:, head_position],
                keys[:, :, key_value_head],
                preferred_element_type=jnp.float32,
            )
            * scaling
        )
        scores = jnp.where(row_live[None], scores, -jnp.inf)
        slot_top = jnp.max(scores, axis=-1)
        clip_top = jnp.max(jnp.where(member[:, None, :], slot_top[None, :, :], -jnp.inf), axis=-1)
        clip_top = jnp.maximum(clip_top, 0.0)
        slot_shift = jnp.take(clip_top, slot_clip, axis=0)
        soft_terms = jnp.exp(scores - jnp.transpose(slot_shift)[..., None])
        slot_total = jnp.sum(soft_terms, axis=-1)
        clip_total = jnp.sum(slot_total[None, :, :] * member_float[:, None, :], axis=-1) + jnp.exp(
            -clip_top
        )
        rounded_result = soft_terms.astype(jnp.bfloat16)
        slot_sums = jnp.einsum(
            "ori,rin->orn",
            rounded_result,
            value_rows[:, :, key_value_head],
            preferred_element_type=jnp.float32,
        )
        clip_sums = jnp.einsum(
            "lsd,cs->cld", slot_sums, member_float, precision=lax.Precision.HIGHEST
        )
        head_parts.append(clip_sums / clip_total[..., None])
    attention = jnp.concatenate(head_parts, axis=-1).astype(jnp.bfloat16)
    mixed = output_folded(attention.reshape(clips_here * lat_rows, width), w_out)
    state = latents.astype(jnp.float32)[None] + mixed.reshape(clips_here, lat_rows, width)
    latent_state = state.astype(jnp.bfloat16)
    pooled = jnp.mean(state, axis=1).astype(jnp.bfloat16)
    embed = embed_folded(pooled, w_proj)
    embed_unit = (embed / jnp.sqrt(jnp.sum(embed * embed, axis=-1, keepdims=True) + 1e-06)).astype(
        jnp.bfloat16
    )
    frames = jnp.take(movie_frame_embeddings, clip_frame, axis=0).astype(jnp.float32)
    frame_unit = (
        frames / jnp.sqrt(jnp.sum(frames * frames, axis=-1, keepdims=True) + 1e-06)
    ).astype(jnp.bfloat16)
    scale_value = logit_scale[0]
    own_pair = scale_value * jnp.sum(
        embed_unit.astype(jnp.float32) * frame_unit.astype(jnp.float32), axis=-1
    )
    smallest_value = jnp.full((clips_here,), -jnp.inf, jnp.float32)
    nothing = jnp.zeros((clips_here,), jnp.float32)
    row_top = smallest_value
    row_sum = nothing
    col_top = smallest_value
    col_sum = nothing
    other_embed = lax.all_gather(embed_unit, ("sess", "dp", "fsdp"), axis=0, tiled=True)
    other_frame = lax.all_gather(frame_unit, ("sess", "dp", "fsdp"), axis=0, tiled=True)
    row_logit = scale_value * jnp.dot(embed_unit, other_frame.T, preferred_element_type=jnp.float32)
    col_logit = scale_value * jnp.dot(frame_unit, other_embed.T, preferred_element_type=jnp.float32)
    row_next = jnp.max(row_logit, axis=1)
    col_next = jnp.max(col_logit, axis=1)
    row_sum = row_sum * jnp.exp(row_top - row_next) + jnp.sum(
        jnp.exp(row_logit - row_next[:, None]), axis=1
    )
    col_sum = col_sum * jnp.exp(col_top - col_next) + jnp.sum(
        jnp.exp(col_logit - col_next[:, None]), axis=1
    )
    row_top, row_sum, col_top, col_sum = (row_next, row_sum, col_next, col_sum)
    clip_loss = 0.5 * (row_top + jnp.log(row_sum) + col_top + jnp.log(col_sum)) - own_pair
    return (latent_state, clip_loss)


def solution(mesh):
    return jax.shard_map(
        per_device,
        mesh=mesh,
        in_specs=(
            P(("sess", "dp", "fsdp"), None, None),
            P(("sess", "dp", "fsdp"), None),
            P(("sess", "dp", "fsdp")),
            P(("sess", "dp", "fsdp")),
            P(),
            P(),
            P("fsdp", None),
            P("fsdp", None),
            P("fsdp", None),
            P(),
            P(("sess", "dp", "fsdp")),
            P(),
        ),
        out_specs=(P(("sess", "dp", "fsdp"), None, None), P(("sess", "dp", "fsdp"))),
        check_vma=False,
    )
```

profile of v0, /device:TPU:8, one launch (start us, length us, event | category | flops | bytes accessed | tf_op | source)
XLA Modules:
  0.0 1890.5 jit_solution(8112834568392189841)
XLA Ops:
  11.1 10.6 all-to-all-start
  21.7 4.8 reshape.604
  26.5 7.1 fusion.134
  33.6 31.8 %copy.220 = bf16[32,2,131072]{2,1,0:T(2,128)(2,1)} copy(bf16[32,2,131072]{2,0,1:T(8,128)(2,1)S(1)} %fusion.134) | data formatting | bytes 33554432 | tf_op jit(solution)/shard_map/bs,bx->sx/dot_general | solution.py:62
  65.4 10.1 all-to-all-start.1
  80.1 366.0 %all-to-all-done.1 = bf16[32,2,131072]{2,1,0:T(2,128)(2,1)} async-done(((bf16[32,2,131072]{2,1,0:T(2,128)(2,1)}), bf16[32,2,131072]{2,1,0:T(2,128)(2,1)}, u32[]{:S(2)}, u32[]{:S(2)}) %all-to-all-start.1) | async-done | bytes 16777248 | tf_op jit(solution)/shard_map/all_to_all | solution.py:70
  446.1 29.1 %reshape.408 = bf16[8192,1024]{1,0:T(8,128)(2,1)} reshape(bf16[32,2,131072]{2,1,0:T(2,128)(2,1)} %all-to-all-done.1) | data formatting | bytes 33554432 | tf_op jit(solution)/shard_map/reshape | solution.py:73
  475.3 12.7 convolution_convert_fusion
  488.0 3.6 fusion.167
  491.6 6.6 copy.310
  498.2 1.7 fusion.185
  500.0 1.7 fusion.171
  501.8 2.7 fusion.172
  504.5 2.6 fusion.173
  507.2 2.6 fusion.174
  509.8 2.6 fusion.175
  512.4 2.6 fusion.176
  515.1 2.6 fusion.177
  517.8 2.6 fusion.178
  520.4 2.6 fusion.179
  523.1 2.6 fusion.180
  525.7 2.6 fusion.181
  528.4 2.6 fusion.182
  531.0 2.6 fusion.183
  533.7 2.6 fusion.184
  536.3 2.6 fusion.170
  548.9 6.8 copy.308
  555.9 2.0 fusion.99
  557.9 3.3 convolution_bitcast_fusion
  561.8 1.7 convolution_bitcast_fusion.1
  564.2 1.7 convolution_bitcast_fusion.2
  566.6 1.7 convolution_bitcast_fusion.3
  568.9 1.7 convolution_bitcast_fusion.4
  571.3 1.7 convolution_bitcast_fusion.5
  573.7 1.8 convolution_bitcast_fusion.6
  576.1 1.7 convolution_bitcast_fusion.7
  578.5 1.7 convolution_bitcast_fusion.8
  580.8 1.9 convolution_bitcast_fusion.9
  583.4 1.7 convolution_bitcast_fusion.10
  585.8 1.7 convolution_bitcast_fusion.11
  588.1 1.7 convolution_bitcast_fusion.12
  590.5 1.7 convolution_bitcast_fusion.13
  592.8 1.8 convolution_bitcast_fusion.14
  598.4 2.3 fusion.52
  600.7 2.3 fusion.51
  603.0 1.0 fusion.50
  604.1 2.3 fusion.49
  606.4 2.5 fusion.48
  608.9 2.3 fusion.47
  611.2 2.3 fusion.46
  613.5 2.2 fusion.45
  615.8 1.0 fusion.44
  616.8 1.0 fusion.43
  617.9 1.0 fusion.42
  618.9 1.0 fusion.41
  620.0 1.0 fusion.40
  621.0 1.0 fusion.39
  622.1 1.0 fusion.38
  623.1 2.0 convolution_bitcast_fusion.15
  625.1 1.3 fusion.37
  627.2 2.7 fusion.168
  629.9 1.6 multiply_reduce_fusion.17
  631.7 623.4 %all-gather = bf16[256,2,512]{2,1,0:T(2,128)(2,1)S(1)} all-gather(bf16[1,2,512]{2,1,0:T(2,128)(2,1)S(1)} %bitcast.394), channel_id=1, replica_groups=mesh['sess'=32,'dp'=4,'fsdp'=2] {'sess','dp','fsdp'}, dimensions={0}, use_global_device_ids=true | all-gather | bytes 526336 | tf_op jit(solution)/shard_map/all_gather | solution.py:145
  1255.3 626.3 %all-gather.1 = bf16[256,2,512]{2,1,0:T(2,128)(2,1)S(1)} all-gather(bf16[1,2,512]{2,1,0:T(2,128)(2,1)S(1)} %bitcast.395), channel_id=1, replica_groups=mesh['sess'=32,'dp'=4,'fsdp'=2] {'sess','dp','fsdp'}, dimensions={0}, use_global_device_ids=true | all-gather | bytes 526336 | tf_op jit(solution)/shard_map/all_gather | solution.py:144
  (215 shorter events, 34.5 us)
Async XLA Ops:
  7.2 71.5 %copy-start = (bf16[512,512]{1,0:T(8,128)(2,1)S(1)}, bf16[512,512]{1,0:T(8,128)(2,1)}, u32[]{:S(2)}) copy-start(bf16[512,512]{1,0:T(8,128)(2,1)} %param.23) | copy-start | bytes 1572868
  11.1 54.3 %all-to-all-start = ((bf16[32,2,2]{1,2,0:T(2,128)(2,1)}), bf16[32,2,2]{1,2,0:T(2,128)(2,1)S(1)}, u32[]{:S(2)}, u32[]{:S(2)}) async-start(bf16[32,2,2]{1,2,0:T(2,128)(2,1)} %copy.217), calls=%async_computation | async-start | bytes 32768 | tf_op jit(solution)/shard_map/all_to_all | solution.py:71
  65.4 12.3 copy-start.24
  65.4 12.5 copy-start.25
  65.4 13.2 copy-start.26
  65.4 380.7 %all-to-all-start.1 = ((bf16[32,2,131072]{2,1,0:T(2,128)(2,1)}), bf16[32,2,131072]{2,1,0:T(2,128)(2,1)}, u32[]{:S(2)}, u32[]{:S(2)}) async-start(bf16[32,2,131072]{2,1,0:T(2,128)(2,1)} %copy.220), calls=%async_computation.1 | async-start | bytes 33554432 | tf_op jit(solution)/shard_map/all_to_all | solution.py:70
  75.5 399.7 %all-gather.6.cloned.1.call-start = ((), (), s32[]{:S(2)}) async-start(), calls=%async_computation.2 | async-start | bytes 1572864 | tf_op jit(solution)/shard_map/all_gather | solution.py:17
  76.3 550.9 %all-gather.8.cloned.1.call-start = ((), (), s32[]{:S(2)}) async-start(), calls=%async_computation.3 | async-start | bytes 3145728 | tf_op jit(solution)/shard_map/all_gather | solution.py:21
  77.0 552.9 %all-gather.10.cloned.1.call-start = ((), (), s32[]{:S(2)}) async-start(), calls=%async_computation.4 | async-start | bytes 1572864 | tf_op jit(solution)/shard_map/all_gather | solution.py:25
  555.7 5.4 copy-start.15
  555.7 6.1 copy-start.2
  555.9 7.7 copy-start.14
  561.1 4.8 copy-start.13
  563.5 4.7 copy-start.12
  565.9 4.7 copy-start.11
  568.3 4.8 copy-start.10
  570.7 4.8 copy-start.9
  573.0 4.8 copy-start.8
  575.5 4.7 copy-start.7
  577.8 5.0 copy-start.6
  580.2 5.0 copy-start.5
  582.8 4.7 copy-start.4
  585.1 4.7 copy-start.3
  594.6 8.4 copy-start.16
  598.4 17.4 copy-start.17
  600.7 16.1 copy-start.18
  603.0 14.8 copy-start.19
  604.1 14.8 copy-start.20
  606.4 13.6 copy-start.21
  608.9 12.1 copy-start.22
  611.2 10.9 copy-start.23
  625.1 1258.4 %copy-start.1 = (bf16[512,512]{1,0:T(8,128)(2,1)S(1)}, bf16[512,512]{1,0:T(8,128)(2,1)}, u32[]{:S(2)}) copy-start(bf16[512,512]{1,0:T(8,128)(2,1)} %param.23) | copy-start | bytes 1572868
Sparse Core Ops, SparseCore 0:
  78.1 54.6 all-gather.5
  134.6 56.9 all-gather.7
  193.4 53.8 all-gather.9
where the time goes:
time: 1900 us; the launch traced here: 1890 us
  blocking collectives  1250 us (66%)
  waiting for transfers between devices  368 us (19%)
  matrix products  120 us (6%)
  local copies, waits for them, and re-layouts  99.2 us (5%)
  starting transfers between devices  20.8 us (1%)
    all_gather x1, blocking collectives, per_device(): lax.all_gather(embed_unit, ('sess', 'dp', 'fsdp'), axis=0, tiled=True)  626 us
    all_gather x1, blocking collectives, per_device(): lax.all_gather(frame_unit, ('sess', 'dp', 'fsdp'), axis=0, tiled=True)  623 us
    all_to_all x1, waiting for transfers between devices, per_device(): lax.all_to_all(packed, 'sess', split_axis=0, concat_axis=0, tiled=True)  366 us
    dot_general x16, matrix products, per_device(): jnp.einsum('wa,pha->wph', query[:, head_position], keys[:, :, key_value_h...  39.7 us
  transfers between devices with their start and end apart: 5, of which 1 were waited for; matrix products, arithmetic and copies ran while one was open for 12% of the time, Pallas kernels for 0%

commit v1 on v0

--- a/solution.py
+++ b/solution.py
@@ -142,7 +142,15 @@
     col_top = smallest_value
     col_sum = nothing
     other_embed = lax.all_gather(embed_unit, ("sess", "dp", "fsdp"), axis=0, tiled=True)
-    other_frame = lax.all_gather(frame_unit, ("sess", "dp", "fsdp"), axis=0, tiled=True)
+    other_frame = jnp.concatenate(
+        lax.all_to_all(
+            jnp.stack([frame_unit] * lax.axis_size(("sess", "dp", "fsdp")), 0),
+            ("sess", "dp", "fsdp"),
+            0,
+            0,
+        ),
+        0,
+    )
     row_logit = scale_value * jnp.dot(embed_unit, other_frame.T, preferred_element_type=jnp.float32)
     col_logit = scale_value * jnp.dot(frame_unit, other_embed.T, preferred_element_type=jnp.float32)
     row_next = jnp.max(row_logit, axis=1)

time: 1900 us -> 1300 us (0.68)
  blocking collectives: 1250 us -> 630 us
    all_gather x1 -> x0, blocking collectives: 623 us -> none  [per_device(): lax.all_gather(frame_unit, ('sess', 'dp', 'fsdp'), axis=0, tiled=True)]
  transfers between devices with their start and end apart: 5 -> 6, of which waited for: 1 -> 1; matrix products, arithmetic and copies ran while one was open for 12% -> 18% of each run, Pallas kernels for 0% -> 0%
where the time goes in v1:
time: 1300 us; the launch traced here: 1290 us
  blocking collectives  630 us (48%)
  waiting for transfers between devices  369 us (28%)
  matrix products  120 us (9%)
  local copies, waits for them, and re-layouts  100 us (8%)
  starting transfers between devices  34.1 us (3%)
  other arithmetic  16.8 us (1%)
  between operations  15.7 us (1%)
    all_gather x1, blocking collectives, per_device(): lax.all_gather(embed_unit, ('sess', 'dp', 'fsdp'), axis=0, tiled=True)  630 us
    all_to_all x1, waiting for transfers between devices, per_device(): lax.all_to_all(packed, 'sess', split_axis=0, concat_axis=0, tiled=True)  367 us
    dot_general x16, matrix products, per_device(): jnp.einsum('wa,pha->wph', query[:, head_position], keys[:, :, key_value_h...  39.7 us
    dot_general x1, local copies, waits for them, and re-layouts, per_device(): jnp.einsum('bs,bx->sx', placing, unit_tokens.reshape(blocks_here, block_r...  31.8 us
    dot_general x16, matrix products, per_device(): jnp.einsum('ori,rin->orn', rounded_result, value_rows[:, :, key_value_hea...  29.6 us
    reshape x1, local copies, waits for them, and re-layouts, per_device(): arrived.reshape(slots_all * block_rows, width)  29.1 us
  transfers between devices with their start and end apart: 6, of which 1 were waited for; matrix products, arithmetic and copies ran while one was open for 18% of the time, Pallas kernels for 0%

profile of v1, /device:TPU:8, one launch (start us, length us, event | category | flops | bytes accessed | tf_op | source)
XLA Modules:
  0.0 1285.9 jit_solution(863729279433101412)
XLA Ops:
  11.1 10.6 all-to-all-start
  21.7 4.8 reshape.620
  26.5 7.1 fusion.134
  33.6 31.8 %copy.220 = bf16[32,2,131072]{2,1,0:T(2,128)(2,1)} copy(bf16[32,2,131072]{2,0,1:T(8,128)(2,1)S(1)} %fusion.134) | data formatting | bytes 33554432 | tf_op jit(solution)/shard_map/bs,bx->sx/dot_general | solution.py:62
  65.4 10.1 all-to-all-start.1
  79.5 366.7 %all-to-all-done.1 = bf16[32,2,131072]{2,1,0:T(2,128)(2,1)} async-done(((bf16[32,2,131072]{2,1,0:T(2,128)(2,1)}), bf16[32,2,131072]{2,1,0:T(2,128)(2,1)}, u32[]{:S(2)}, u32[]{:S(2)}) %all-to-all-start.1) | async-done | bytes 16777248 | tf_op jit(solution)/shard_map/all_to_all | solution.py:70
  446.1 29.1 %reshape.425 = bf16[8192,1024]{1,0:T(8,128)(2,1)} reshape(bf16[32,2,131072]{2,1,0:T(2,128)(2,1)} %all-to-all-done.1) | data formatting | bytes 33554432 | tf_op jit(solution)/shard_map/reshape | solution.py:73
  475.3 12.7 convolution_convert_fusion
  488.0 3.6 fusion.167
  491.6 6.6 copy.310
  498.2 1.7 fusion.185
  500.0 1.7 fusion.171
  501.8 2.7 fusion.172
  504.5 2.6 fusion.173
  507.2 2.6 fusion.174
  509.8 2.6 fusion.175
  512.4 2.6 fusion.176
  515.1 2.6 fusion.177
  517.8 2.6 fusion.178
  520.4 2.6 fusion.179
  523.1 2.6 fusion.180
  525.7 2.6 fusion.181
  528.4 2.6 fusion.182
  531.0 2.6 fusion.183
  533.7 2.6 fusion.184
  536.3 2.6 fusion.170
  548.9 6.8 copy.308
  555.9 2.0 fusion.99
  557.9 3.3 convolution_bitcast_fusion
  561.8 1.7 convolution_bitcast_fusion.1
  564.2 1.7 convolution_bitcast_fusion.2
  566.6 1.7 convolution_bitcast_fusion.3
  568.9 1.7 convolution_bitcast_fusion.4
  571.3 1.7 convolution_bitcast_fusion.5
  573.7 1.8 convolution_bitcast_fusion.6
  576.1 1.7 convolution_bitcast_fusion.7
  578.5 1.7 convolution_bitcast_fusion.8
  580.8 1.9 convolution_bitcast_fusion.9
  583.4 1.7 convolution_bitcast_fusion.10
  585.8 1.7 convolution_bitcast_fusion.11
  588.1 1.7 convolution_bitcast_fusion.12
  590.5 1.7 convolution_bitcast_fusion.13
  592.8 1.8 convolution_bitcast_fusion.14
  598.4 2.3 fusion.52
  600.7 2.3 fusion.51
  603.0 1.0 fusion.50
  604.1 2.3 fusion.49
  606.4 2.5 fusion.48
  608.9 2.3 fusion.47
  611.2 2.3 fusion.46
  613.5 2.2 fusion.45
  615.8 1.0 fusion.44
  616.8 1.0 fusion.43
  617.9 1.0 fusion.42
  618.9 1.0 fusion.41
  620.0 1.0 fusion.40
  621.0 1.0 fusion.39
  623.1 2.0 convolution_bitcast_fusion.15
  625.1 1.3 fusion.37
  627.2 2.7 fusion.168
  629.9 1.6 multiply_reduce_fusion.17
  631.7 1.1 stack.14
  632.8 13.3 %all-to-all-start.2 = ((bf16[256,2,512]{2,1,0:T(2,128)(2,1)}), bf16[256,2,512]{2,1,0:T(2,128)(2,1)S(1)}, u32[]{:S(2)}, u32[]{:S(2)}) async-start(bf16[256,2,512]{2,1,0:T(2,128)(2,1)} %stack.14), calls=%async_computation.2 | async-start | bytes 1048576 | tf_op jit(solution)/shard_map/all_to_all | solution.py:146
  646.7 630.1 %all-gather = bf16[256,2,512]{2,1,0:T(2,128)(2,1)S(1)} all-gather(bf16[1,2,512]{2,1,0:T(2,128)(2,1)S(1)} %bitcast.393), channel_id=1, replica_groups=mesh['sess'=32,'dp'=4,'fsdp'=2] {'sess','dp','fsdp'}, dimensions={0}, use_global_device_ids=true | all-gather | bytes 526336 | tf_op jit(solution)/shard_map/all_gather | solution.py:144
  (217 shorter events, 35.5 us)
Async XLA Ops:
  7.2 70.8 %copy-start = (bf16[512,512]{1,0:T(8,128)(2,1)S(1)}, bf16[512,512]{1,0:T(8,128)(2,1)}, u32[]{:S(2)}) copy-start(bf16[512,512]{1,0:T(8,128)(2,1)} %param.23) | copy-start | bytes 1572868
  11.1 54.3 %all-to-all-start = ((bf16[32,2,2]{1,2,0:T(2,128)(2,1)}), bf16[32,2,2]{1,2,0:T(2,128)(2,1)S(1)}, u32[]{:S(2)}, u32[]{:S(2)}) async-start(bf16[32,2,2]{1,2,0:T(2,128)(2,1)} %copy.217), calls=%async_computation | async-start | bytes 32768 | tf_op jit(solution)/shard_map/all_to_all | solution.py:71
  65.4 12.3 copy-start.24
  65.4 12.5 copy-start.25
  65.4 12.5 copy-start.26
  65.4 380.7 %all-to-all-start.1 = ((bf16[32,2,131072]{2,1,0:T(2,128)(2,1)}), bf16[32,2,131072]{2,1,0:T(2,128)(2,1)}, u32[]{:S(2)}, u32[]{:S(2)}) async-start(bf16[32,2,131072]{2,1,0:T(2,128)(2,1)} %copy.220), calls=%async_computation.1 | async-start | bytes 33554432 | tf_op jit(solution)/shard_map/all_to_all | solution.py:70
  75.5 399.7 %all-gather.5.cloned.1.call-start = ((), (), s32[]{:S(2)}) async-start(), calls=%async_computation.3 | async-start | bytes 1572864 | tf_op jit(solution)/shard_map/all_gather | solution.py:17
  76.3 550.9 %all-gather.7.cloned.1.call-start = ((), (), s32[]{:S(2)}) async-start(), calls=%async_computation.4 | async-start | bytes 3145728 | tf_op jit(solution)/shard_map/all_gather | solution.py:21
  77.0 552.9 %all-gather.9.cloned.1.call-start = ((), (), s32[]{:S(2)}) async-start(), calls=%async_computation.5 | async-start | bytes 1572864 | tf_op jit(solution)/shard_map/all_gather | solution.py:25
  555.7 5.4 copy-start.15
  555.7 6.1 copy-start.2
  555.9 7.7 copy-start.14
  561.1 4.8 copy-start.13
  563.5 4.7 copy-start.12
  565.9 4.7 copy-start.11
  568.3 4.8 copy-start.10
  570.7 4.8 copy-start.9
  573.0 4.8 copy-start.8
  575.5 4.7 copy-start.7
  577.8 5.0 copy-start.6
  580.2 5.0 copy-start.5
  582.8 4.7 copy-start.4
  585.1 4.7 copy-start.3
  594.6 8.4 copy-start.16
  598.4 17.4 %copy-start.17 = (f32[32,64,64]{2,0,1:T(8,128)S(1)}, f32[32,64,64]{2,0,1:T(8,128)}, u32[]{:S(2)}) copy-start(f32[32,64,64]{2,0,1:T(8,128)} %convolution_bitcast_fusion.8) | copy-start | bytes 1572868
  600.7 16.1 %copy-start.18 = (f32[32,64,64]{2,0,1:T(8,128)S(1)}, f32[32,64,64]{2,0,1:T(8,128)}, u32[]{:S(2)}) copy-start(f32[32,64,64]{2,0,1:T(8,128)} %convolution_bitcast_fusion.9) | copy-start | bytes 1572868
  603.0 14.8 %copy-start.19 = (f32[32,64,64]{2,0,1:T(8,128)S(1)}, f32[32,64,64]{2,0,1:T(8,128)}, u32[]{:S(2)}) copy-start(f32[32,64,64]{2,0,1:T(8,128)} %convolution_bitcast_fusion.10) | copy-start | bytes 1572868
  604.1 14.8 %copy-start.20 = (f32[32,64,64]{2,0,1:T(8,128)S(1)}, f32[32,64,64]{2,0,1:T(8,128)}, u32[]{:S(2)}) copy-start(f32[32,64,64]{2,0,1:T(8,128)} %convolution_bitcast_fusion.11) | copy-start | bytes 1572868
  606.4 13.6 %copy-start.21 = (f32[32,64,64]{2,0,1:T(8,128)S(1)}, f32[32,64,64]{2,0,1:T(8,128)}, u32[]{:S(2)}) copy-start(f32[32,64,64]{2,0,1:T(8,128)} %convolution_bitcast_fusion.12) | copy-start | bytes 1572868
  608.9 12.1 copy-start.22
  611.2 10.9 copy-start.23
  626.4 652.5 %copy-start.1 = (bf16[512,512]{1,0:T(8,128)(2,1)S(1)}, bf16[512,512]{1,0:T(8,128)(2,1)}, u32[]{:S(2)}) copy-start(bf16[512,512]{1,0:T(8,128)(2,1)} %param.23) | copy-start | bytes 1572868
  632.8 644.8 %all-to-all-start.2 = ((bf16[256,2,512]{2,1,0:T(2,128)(2,1)}), bf16[256,2,512]{2,1,0:T(2,128)(2,1)S(1)}, u32[]{:S(2)}, u32[]{:S(2)}) async-start(bf16[256,2,512]{2,1,0:T(2,128)(2,1)} %stack.14), calls=%async_computation.2 | async-start | bytes 1048576 | tf_op jit(solution)/shard_map/all_to_all | solution.py:146
Sparse Core Ops, SparseCore 0:
  78.1 54.6 all-gather.4
  134.6 56.9 all-gather.6
  193.4 53.8 all-gather.8
